TPU v7x, 128 devices: a whole 4x4x4 slice. The times are simulated.
128 devices in a mesh: grp: 32 (over y, x, core), mem: 4 (over z).
Axes of the slice: x: 4, y: 4, z: 4, core: 2. Of those that a mesh axis runs over, the one named last changes fastest.
Arguments:
- incident: bfloat16 [2, 256, 65536], P(None, None, ('grp', 'mem')), may hold values from -6 to 6
- near_blocks: bfloat16 [256, 3, 2, 256, 256], P(('grp', 'mem')), may hold values from -0.15625 to 0.15625
- near_mask: int32 [256, 3], P(('grp', 'mem')), may hold values 0 or 1
- far_source: int32 [32, 14], replicated, may hold values from 0 to 31
- far_rank: int32 [32, 14], P('grp'), may hold values from 32 to 128
- basis_in: bfloat16 [32, 4, 14, 2, 128, 512], P('grp', 'mem'), may hold values from -0.1875 to 0.1875
- section_one: bfloat16 [32, 4, 14, 2, 128, 256], P('grp', 'mem'), may hold values from -0.25 to 0.25
- section_two: bfloat16 [32, 4, 14, 2, 128, 256], P('grp', 'mem'), may hold values from -0.25 to 0.25
- basis_out: bfloat16 [32, 4, 14, 2, 2048, 128], P('grp', 'mem'), may hold values from -0.0625 to 0.0625
Outputs:
- product: bfloat16 [2, 256, 65536], P(None, None, ('grp', 'mem'))
Inputs may be any that keep to these rules, and one draw needn't show every extreme that they name: far_source names the cluster whose coefficients feed each far-field block; clusters may repeat. far_rank gives the number of live rank components of each block. `near_mask`: 1 marks a present near-field block.
All inputs are finite; a program needn't handle non-finite values.
Results may differ from a plain program's by a relative error of at most 0.0053.
Values may be sent and summed in bfloat16 or wider, within the bound.
No kernel may reach another device: no remote copies, remote signals or barrier semaphores. Data moves between devices by JAX's collectives and lax.ppermute only.
A program may use at most 128 MiB of HBM per device.

v0:
```python
import jax
import jax.numpy as jnp
from jax import lax
from jax.sharding import PartitionSpec as P


def with_halo(block, sides, width):
    for axis, dim in sides:
        count = lax.axis_size(axis)
        forward = [(i, i + 1) for i in range(count - 1)]
        backward = [(target, source) for source, target in forward]
        low = lax.ppermute(
            lax.slice_in_dim(block, block.shape[dim] - width, None, axis=dim), axis, forward
        )
        high = lax.ppermute(lax.slice_in_dim(block, 0, width, axis=dim), axis, backward)
        block = jnp.concatenate([low, block, high], axis=dim)
    return block


def partner_2(value, axis, stride):
    return lax.ppermute(value, axis, [(i, i ^ 1 << stride) for i in range(lax.axis_size(axis))])


def complex_apply(weight_real, weight_imag, vector_real, vector_imag, form):

    def mult(left, right):
        return jnp.einsum(form, left, right, preferred_element_type=jnp.float32)

    first = mult(weight_real, vector_real) - mult(weight_imag, vector_imag)
    second = mult(weight_real, vector_imag) + mult(weight_imag, vector_real)
    return (first, second)


def mix_section(level, partner, upper_bit, weights, keep):
    is_upper = upper_bit == 1
    lower_half = jnp.where(is_upper, partner, level)
    upper_half = jnp.where(is_upper, level, partner)
    joined = jnp.concatenate([lower_half, upper_half], -1)
    first, second = complex_apply(
        weights[:, 0], weights[:, 1], joined[:, 0], joined[:, 1], "fkj,fnj->fnk"
    )
    return jnp.stack([first * keep, second * keep], 1).astype(jnp.bfloat16)


def on_device(
    incident,
    near_blocks,
    near_mask,
    far_source,
    far_rank,
    basis_in,
    section_one,
    section_two,
    basis_out,
):
    nrhs_count = incident.shape[1]
    row_count = incident.shape[2]
    leaf_size = near_blocks.shape[3]
    leaf_count = near_blocks.shape[0]
    rank_size = basis_in.shape[4]
    group = lax.axis_index("grp")
    member = lax.axis_index("mem")
    sources = lax.dynamic_slice_in_dim(far_source, group, 1, 0)[0]
    arrived = lax.all_gather(incident[None], "grp", axis=0, tiled=True)
    chosen = jnp.take(arrived, sources, axis=0)
    padded = with_halo(incident, ((("grp", "mem"), 2),), leaf_size)
    near_real = jnp.zeros((nrhs_count, leaf_count, leaf_size), jnp.float32)
    near_imag = jnp.zeros((nrhs_count, leaf_count, leaf_size), jnp.float32)
    for offset in range(3):
        window = padded[:, :, offset * leaf_size : offset * leaf_size + row_count].reshape(
            2, nrhs_count, leaf_count, leaf_size
        )
        first, second = complex_apply(
            near_blocks[:, offset, 0],
            near_blocks[:, offset, 1],
            window[0],
            window[1],
            "lab,nlb->nla",
        )
        weight = near_mask[:, offset].astype(jnp.float32)[None, :, None]
        near_real = near_real + weight * first
        near_imag = near_imag + weight * second
    near = jnp.stack(
        [near_real.reshape(nrhs_count, row_count), near_imag.reshape(nrhs_count, row_count)], 0
    )
    keep = (jnp.arange(rank_size)[None, :] < far_rank[0][:, None]).astype(jnp.float32)[:, None, :]
    factor = basis_in[0, 0]
    first, second = complex_apply(
        factor[:, 0], factor[:, 1], chosen[:, 0], chosen[:, 1], "fkr,fnr->fnk"
    )
    level = jnp.stack([first * keep, second * keep], 1).astype(jnp.bfloat16)
    partner = partner_2(level, "mem", 0)
    level = mix_section(level, partner, member % 2, section_one[0, 0], keep)
    partner = partner_2(level, "mem", 1)
    level = mix_section(level, partner, member // 2 % 2, section_two[0, 0], keep)
    outward = basis_out[0, 0]
    first, second = complex_apply(
        outward[:, 0], outward[:, 1], level[:, 0], level[:, 1], "frk,fnk->nr"
    )
    terms = jnp.stack([first, second], 0)
    far = lax.psum_scatter(terms, "mem", scatter_dimension=2, tiled=True)
    return (far + near).astype(jnp.bfloat16)


def solution(mesh):
    placed = (
        P(None, None, ("grp", "mem")),
        P(("grp", "mem"), None, None, None, None),
        P(("grp", "mem"), None),
        P(),
        P("grp", None),
        P("grp", "mem", None, None, None, None),
        P("grp", "mem", None, None, None, None),
        P("grp", "mem", None, None, None, None),
        P("grp", "mem", None, None, None, None),
    )
    return jax.shard_map(
        on_device,
        mesh=mesh,
        in_specs=placed,
        out_specs=P(None, None, ("grp", "mem")),
        check_vma=False,
    )
```

profile of v0, /device:TPU:7, one launch (start us, length us, event | category | flops | bytes accessed | tf_op | source)
XLA Modules:
  0.0 273.7 jit_solution(2111088577205598691)
XLA Ops:
  7.3 4.4 %copy.174 = bf16[1,1,14,2,128,512]{5,4,2,3,1,0:T(8,128)(2,1)} copy(bf16[1,1,14,2,128,512]{5,4,3,2,1,0:T(8,128)(2,1)} %param.14) | data formatting | bytes 7340032 | tf_op args[5]
  12.0 72.8 %all-gather.3.cloned.1.call-done = bf16[64,256,512]{2,1,0:T(8,128)(2,1)} async-done(((bf16[2,256,512]{2,1,0:T(8,128)(2,1)}), bf16[64,256,512]{2,1,0:T(8,128)(2,1)}) %all-gather.3.cloned.1.call-update) | async-done | bytes 16777232 | tf_op jit(solution)/shard_map/all_gather | solution.py:64
  84.8 10.2 %gather_fusion = bf16[14,2,256,512]{3,2,1,0:T(8,128)(2,1)} fusion(bf16[32,2,256,512]{3,2,1,0:T(8,128)(2,1)} %bitcast.224, s32[1024]{0:T(1024)S(1)} %pad_clamp_fusion), kind=kCustom, calls=%fused_computation | custom fusion | bytes 14680120 | tf_op jit(solution)/shard_map/jit(_take)/gather | solution.py:65
  95.0 4.0 %copy_select_fusion = bf16[14,2,256,512]{3,2,0,1:T(8,128)(2,1)S(1)} fusion(bf16[14,2,256,512]{3,2,1,0:T(8,128)(2,1)} %gather_fusion, pred[14]{0:T(512)(128)(4,1)S(1)} %compare_and_fusion), kind=kLoop, calls=%fused_computation.4 | loop fusion | flops 3670016 | bytes 14680078 | tf_op jit(solution)/shard_map/jit(_take)/select_n | solution.py:65
  107.5 1.7 copy.176
  109.2 38.7 %collective-permute-done = bf16[14,2,256,128]{2,3,0,1:T(8,128)(2,1)} collective-permute-done((bf16[14,2,256,128]{2,3,0,1:T(8,128)(2,1)}, bf16[14,2,256,128]{2,3,0,1:T(8,128)(2,1)}, u32[]{:S(2)}, u32[]{:S(2)}) %collective-permute-start) | collective-permute-done | bytes 1835040 | tf_op jit(solution)/shard_map/ppermute | solution.py:21
  147.9 2.0 broadcast_select_fusion
  153.5 2.9 %collective-permute-start.1 = (bf16[14,2,256,128]{2,3,0,1:T(8,128)(2,1)}, bf16[14,2,256,128]{2,3,0,1:T(8,128)(2,1)}, u32[]{:S(2)}, u32[]{:S(2)}) collective-permute-start(bf16[14,2,256,128]{2,3,0,1:T(8,128)(2,1)} %pad_maximum_fusion.4), channel_id=1, source_target_pairs={{0,2},{1,3},{2,0},{3,1},{4,6},{5,7},{6,4},{7,5},{8,10},{9,11},{10,... | collective-permute-start | bytes 5505032 | tf_op jit(solution)/shard_map/ppermute | solution.py:21
  156.4 1.7 copy.175
  158.1 7.3 %copy.173 = bf16[1,1,14,2,2048,128]{5,4,2,3,1,0:T(8,128)(2,1)S(1)} copy(bf16[1,1,14,2,2048,128]{5,4,3,2,1,0:T(8,128)(2,1)} %param.17) | data formatting | bytes 29360128 | tf_op args[8]
  165.4 30.4 %collective-permute-done.1 = bf16[14,2,256,128]{2,3,0,1:T(8,128)(2,1)} collective-permute-done((bf16[14,2,256,128]{2,3,0,1:T(8,128)(2,1)}, bf16[14,2,256,128]{2,3,0,1:T(8,128)(2,1)}, u32[]{:S(2)}, u32[]{:S(2)}) %collective-permute-start.1) | collective-permute-done | bytes 1835040 | tf_op jit(solution)/shard_map/ppermute | solution.py:21
  195.8 2.0 broadcast_select_fusion.3
  200.0 2.1 fusion.9
  202.1 2.1 fusion.8
  204.2 2.1 fusion.13
  206.4 2.1 fusion.15
  208.5 2.2 pad_maximum_fusion
  212.0 6.5 %collective-permute-start.3 = (bf16[2,256,256]{1,2,0:T(8,128)(2,1)S(1)}, bf16[2,256,256]{1,2,0:T(8,128)(2,1)S(1)}, u32[]{:S(2)}, u32[]{:S(2)}) collective-permute-start(bf16[2,256,256]{1,2,0:T(8,128)(2,1)S(1)} %get-tuple-element.20), channel_id=1, source_target_pairs={{1,0},{2,1},{3,2},{4,3},{5,4},{6,5},{7,6},{8,7},{9,8},{10,9},{11,1... | collective-permute-start | bytes 786440 | tf_op jit(solution)/shard_map/ppermute | solution.py:15
  218.6 1.9 collective-permute-start.2
  220.7 6.6 %collective-permute-done.3 = bf16[2,256,256]{1,2,0:T(8,128)(2,1)S(1)} collective-permute-done((bf16[2,256,256]{1,2,0:T(8,128)(2,1)S(1)}, bf16[2,256,256]{1,2,0:T(8,128)(2,1)S(1)}, u32[]{:S(2)}, u32[]{:S(2)}) %collective-permute-start.3) | collective-permute-done | bytes 262176 | tf_op jit(solution)/shard_map/ppermute | solution.py:15
  227.3 8.1 %collective-permute-done.2 = bf16[2,256,256]{1,2,0:T(8,128)(2,1)S(1)} collective-permute-done((bf16[2,256,256]{1,2,0:T(8,128)(2,1)S(1)}, bf16[2,256,256]{1,2,0:T(8,128)(2,1)S(1)}, u32[]{:S(2)}, u32[]{:S(2)}) %collective-permute-start.2) | collective-permute-done | bytes 262176 | tf_op jit(solution)/shard_map/ppermute | solution.py:12
  237.8 2.1 copy.161
  241.5 23.1 %reduce-scatter.2.cloned.1.call-done = f32[2,256,512]{2,1,0:T(8,128)} async-done(((f32[2,256,2048]{2,1,0:T(8,128)}), f32[2,256,512]{2,1,0:T(8,128)}) %reduce-scatter.2.cloned.1.call-update) | async-done | bytes 1048592 | tf_op jit(solution)/shard_map/reduce_scatter | solution.py:101
  264.6 2.2 fusion.35
  (61 shorter events, 20.8 us)
Async XLA Ops:
  6.5 5.1 %copy-start = (s32[32,14]{0,1:T(8,128)S(1)}, s32[32,14]{0,1:T(8,128)}, u32[]{:S(2)}) copy-start(s32[32,14]{0,1:T(8,128)} %param.12) | copy-start | bytes 5380
  6.5 78.2 %all-gather.3.cloned.1.call-start = ((), (), s32[]{:S(2)}) async-start(), calls=%async_computation.2 | async-start | bytes 17301504 | tf_op jit(solution)/shard_map/all_gather | solution.py:64
  7.3 257.4 %reduce-scatter.2.cloned.1.call-start = ((), (), s32[]{:S(2)}) async-start(), calls=%async_computation.1 | async-start | bytes 5242880 | tf_op jit(solution)/shard_map/reduce_scatter | solution.py:101
  7.3 4.6 %copy-start.9 = (s32[1,14]{1,0:T(1,128)S(1)}, s32[1,14]{1,0:T(1,128)}, u32[]{:S(2)}) copy-start(s32[1,14]{1,0:T(1,128)} %param.13) | copy-start | bytes 172
  95.0 4.1 %copy-start.3 = (bf16[1,1,14,2,128,512]{5,4,2,3,1,0:T(8,128)(2,1)S(1)}, bf16[1,1,14,2,128,512]{5,4,2,3,1,0:T(8,128)(2,1)}, u32[]{:S(2)}) copy-start(bf16[1,1,14,2,128,512]{5,4,2,3,1,0:T(8,128)(2,1)} %copy.174) | copy-start | bytes 11010052
  106.3 41.6 %collective-permute-start = (bf16[14,2,256,128]{2,3,0,1:T(8,128)(2,1)}, bf16[14,2,256,128]{2,3,0,1:T(8,128)(2,1)}, u32[]{:S(2)}, u32[]{:S(2)}) collective-permute-start(bf16[14,2,256,128]{2,3,0,1:T(8,128)(2,1)} %pad_maximum_fusion.3), channel_id=1, source_target_pairs={{0,1},{1,0},{2,3},{3,2},{4,5},{5,4},{6,7},{7,6},{8,9},{9,8},{10,11... | collective-permute-start | bytes 5505032 | tf_op jit(solution)/shard_map/ppermute | solution.py:21
  153.5 42.3 %collective-permute-start.1 = (bf16[14,2,256,128]{2,3,0,1:T(8,128)(2,1)}, bf16[14,2,256,128]{2,3,0,1:T(8,128)(2,1)}, u32[]{:S(2)}, u32[]{:S(2)}) collective-permute-start(bf16[14,2,256,128]{2,3,0,1:T(8,128)(2,1)} %pad_maximum_fusion.4), channel_id=1, source_target_pairs={{0,2},{1,3},{2,0},{3,1},{4,6},{5,7},{6,4},{7,5},{8,10},{9,11},{10,... | collective-permute-start | bytes 5505032 | tf_op jit(solution)/shard_map/ppermute | solution.py:21
  210.7 1.0 copy-start.7
  211.8 8.7 %copy-start.8 = (s32[2,3]{1,0:T(2,128)S(1)}, s32[2,3]{1,0:T(2,128)}, u32[]{:S(2)}) copy-start(s32[2,3]{1,0:T(2,128)} %param.11) | copy-start | bytes 76
  212.0 23.5 %copy-start.2 = (bf16[2,3,2,256,256]{4,3,2,1,0:T(8,128)(2,1)S(1)}, bf16[2,3,2,256,256]{4,3,2,1,0:T(8,128)(2,1)}, u32[]{:S(2)}) copy-start(bf16[2,3,2,256,256]{4,3,2,1,0:T(8,128)(2,1)} %param.10) | copy-start | bytes 4718596
  212.0 15.3 %collective-permute-start.3 = (bf16[2,256,256]{1,2,0:T(8,128)(2,1)S(1)}, bf16[2,256,256]{1,2,0:T(8,128)(2,1)S(1)}, u32[]{:S(2)}, u32[]{:S(2)}) collective-permute-start(bf16[2,256,256]{1,2,0:T(8,128)(2,1)S(1)} %get-tuple-element.20), channel_id=1, source_target_pairs={{1,0},{2,1},{3,2},{4,3},{5,4},{6,5},{7,6},{8,7},{9,8},{10,9},{11,1... | collective-permute-start | bytes 786440 | tf_op jit(solution)/shard_map/ppermute | solution.py:15
  218.6 16.8 %collective-permute-start.2 = (bf16[2,256,256]{1,2,0:T(8,128)(2,1)S(1)}, bf16[2,256,256]{1,2,0:T(8,128)(2,1)S(1)}, u32[]{:S(2)}, u32[]{:S(2)}) collective-permute-start(bf16[2,256,256]{1,2,0:T(8,128)(2,1)S(1)} %get-tuple-element.21), channel_id=1, source_target_pairs={{0,1},{1,2},{2,3},{3,4},{4,5},{5,6},{6,7},{7,8},{8,9},{9,10},{10,1... | collective-permute-start | bytes 786440 | tf_op jit(solution)/shard_map/ppermute | solution.py:12
  235.5 1.0 copy-start.4
  236.7 3.4 %copy-start.5 = (bf16[1,256,512]{1,2,0:T(8,128)(2,1)S(1)}, bf16[1,256,512]{1,2,0:T(8,128)(2,1)}, u32[]{:S(2)}) copy-start(bf16[1,256,512]{1,2,0:T(8,128)(2,1)} %copy-done.4) | copy-start | bytes 786436
  241.0 23.6 %copy-start.6 = (f32[1,256,512]{2,1,0:T(8,128)S(1)}, f32[1,256,512]{2,1,0:T(8,128)}, u32[]{:S(2)}) copy-start(f32[1,256,512]{2,1,0:T(8,128)} %copy.161) | copy-start | bytes 1572868
  241.3 25.6 %copy-start.1 = (s32[32,14]{0,1:T(8,128)S(1)}, s32[32,14]{0,1:T(8,128)}, u32[]{:S(2)}) copy-start(s32[32,14]{0,1:T(8,128)} %param.12) | copy-start | bytes 5380
Sparse Core Ops, SparseCore 0:
  9.6 75.1 all-gather.2
  210.9 53.7 reduce-scatter.1
where the time goes:
time: 274 us
  waiting for transfers between devices  180 us (66%)
  local copies, waits for them, and re-layouts  29.1 us (11%)
  matrix products  22.1 us (8%)
  other arithmetic  15.7 us (6%)
  between operations  13.8 us (5%)
  starting transfers between devices  12.6 us (5%)
    all_gather x1, waiting for transfers between devices, on_device(): arrived = lax.all_gather(incident[None], 'grp', axis=0, tiled=True)  72.8 us
    ppermute x2, waiting for transfers between devices, partner_2(): lax.ppermute(value, axis, [(i, i ^ 1 << stride) for i in range(lax.axis_s...  69.1 us
    reduce_scatter x1, waiting for transfers between devices, on_device(): far = lax.psum_scatter(terms, 'mem', scatter_dimension=2, tiled=True)  23.1 us
    dot_general x28, matrix products, mult(): return jnp.einsum(form, left, right, preferred_element_type=jnp.float32)  22.1 us
    unnamed x25, local copies, waits for them, and re-layouts  16.4 us
    gather x1, local copies, waits for them, and re-layouts, on_device(): chosen = jnp.take(arrived, sources, axis=0)  10.2 us
    ppermute x1, waiting for transfers between devices, with_halo(): lax.ppermute(lax.slice_in_dim(block, block.shape[dim] - width, None, axis...  8.07 us
    ppermute x1, waiting for transfers between devices, with_halo(): lax.ppermute(lax.slice_in_dim(block, 0, width, axis=dim), axis, backward)  6.56 us
  transfers between devices with their start and end apart: 6, of which 6 were waited for; matrix products, arithmetic and copies ran while one was open for 8% of the time, Pallas kernels for 0%

commit v1 on v0

v1 whole, which is shorter than its diff:
```python
import functools

import jax
import jax.numpy as jnp
from jax import lax
from jax.experimental import pallas as pl
from jax.experimental.pallas import tpu as pltpu
from jax.sharding import PartitionSpec as P


F32 = jnp.float32
BF16 = jnp.bfloat16
SIDE = 4
SHIFT = {"x": 1, "y": 3}


def swap(value, axis, mask):
    return lax.ppermute(value, axis, [(i, i ^ mask) for i in range(lax.axis_size(axis))])


def ring(value, axis, by):
    at = SHIFT[axis]
    perm = []
    for i in range(lax.axis_size("grp")):
        v = (i >> at) & (SIDE - 1)
        perm.append((i, i + ((((v + by) % SIDE) - v) << at)))
    return lax.ppermute(value, "grp", perm)


def nt(left, right):
    return lax.dot_general(left, right, (((1,), (1,)), ((), ())), preferred_element_type=F32)


VMEM = pl.BlockSpec(memory_space=pltpu.VMEM)
SMEM = pl.BlockSpec(memory_space=pltpu.SMEM)


def size(v):
    return v.size * v.dtype.itemsize


def call(body, scalars, arrays, out_shape, flops, nbytes, scratch=()):
    room = sum(size(v) for v in (*arrays, *jax.tree.leaves(out_shape))) + (2 << 20)
    return pl.pallas_call(
        body,
        in_specs=[SMEM] * len(scalars) + [VMEM] * len(arrays),
        out_specs=jax.tree.map(lambda _: VMEM, out_shape),
        out_shape=out_shape,
        scratch_shapes=scratch,
        compiler_params=pltpu.CompilerParams(vmem_limit_bytes=room),
        cost_estimate=pl.CostEstimate(flops=flops, bytes_accessed=nbytes, transcendentals=0),
    )(*scalars, *arrays)


def near_body(mask, x, low, high, blocks, out):
    nrhs = x.shape[1]
    leaf = blocks.shape[-1]
    rows = nrhs // 4

    def step(t, carry):
        at = pl.ds(pl.multiple_of(t * rows, rows), rows)
        seq = [low[:, at, :]]
        seq += [x[:, at, i * leaf : (i + 1) * leaf] for i in range(2)]
        seq += [high[:, at, :]]
        seq = [v.reshape(2 * rows, leaf) for v in seq]
        for i in range(2):
            real = jnp.zeros((rows, leaf), F32)
            imag = jnp.zeros((rows, leaf), F32)
            for j in range(3):
                p = nt(seq[i + j], blocks[i, j].reshape(2 * leaf, leaf))
                w = mask[i, j].astype(F32)
                real += w * (p[:rows, :leaf] - p[rows:, leaf:])
                imag += w * (p[rows:, :leaf] + p[:rows, leaf:])
            out[0, at, i * leaf : (i + 1) * leaf] = real
            out[1, at, i * leaf : (i + 1) * leaf] = imag
        return carry

    lax.fori_loop(0, 4, step, 0)


def near_field(mask, x, low, high, blocks):
    _, nrhs, rows = x.shape
    leaf = blocks.shape[-1]
    return call(
        near_body, [mask], [x, low, high, blocks],
        jax.ShapeDtypeStruct((2, nrhs, rows), F32),
        8 * nrhs * 6 * leaf * leaf, 4 << 20,
    )


def level0_body(color, base, count, src, gidx, rank, *refs):
    bufs, w, out, xs = refs[:10], refs[10], refs[11], refs[12]
    me = gidx[0]
    k = w.shape[-2]
    n = xs.shape[1]

    def step(i, carry):
        f = i + base
        s = src[me, f]
        dx = (((s >> 1) & 3) - ((me >> 1) & 3)) & 3
        dy = (((s >> 3) & 3) - ((me >> 3) & 3)) & 3
        first, second = (dx, dy) if color == 0 else (dy, dx)
        p = jnp.where(first == 0, 0, jnp.where(first == 3, 1, first + 1))
        b = jnp.where(second == 0, 0, jnp.where(second == 3, 1, jnp.where(second == 1, 2, 3 + (p >> 1))))
        at = jnp.where(b >= 3, p & 1, p)
        which = b + 5 * ((s ^ me) & 1)
        for t in range(10):

            @pl.when(which == t)
            def _():
                xs[...] = bufs[t][at]

        x = xs[...].reshape(2 * n, xs.shape[2])
        p = nt(x, w[0, 0, f].reshape(2 * k, w.shape[-1]))
        live = lax.broadcasted_iota(jnp.int32, (n, k), 1) < rank[0, f]
        real, imag = combine(p, n, k, live)
        out[i, 0] = real
        out[i, 1] = imag
        return carry

    lax.fori_loop(0, count, step, 0)


def level0(color, base, count, src, gidx, rank, bufs, w):
    _, _, n, rows = bufs[0].shape
    k = w.shape[-2]
    return call(
        functools.partial(level0_body, color, base, count),
        [src, gidx, rank], [*bufs, w],
        jax.ShapeDtypeStruct((count, 2, n, k), BF16),
        8 * count * n * k * rows, 2 << 20,
        [pltpu.VMEM((2, n, rows), BF16)],
    )


def combine(p, n, k, live):
    zero = jnp.zeros((n, k), F32)
    real = jnp.where(live, p[:n, :k] - p[n:, k:], zero).astype(BF16)
    imag = jnp.where(live, p[n:, :k] + p[:n, k:], zero).astype(BF16)
    return real, imag


def section_body(base, bit, rank, own, other, *refs):
    half = len(refs) // 2
    ws, outs = refs[:half], refs[half:]
    count, _, n, k = own.shape
    upper = bit[0] == 1
    for i in range(count):
        a = own[i].reshape(2 * n, k)
        b = other[i].reshape(2 * n, k)
        x = jnp.concatenate([jnp.where(upper, b, a), jnp.where(upper, a, b)], axis=1)
        live = lax.broadcasted_iota(jnp.int32, (n, k), 1) < rank[0, base + i]
        for w, out in zip(ws, outs):
            p = nt(x, w[0, 0, base + i].reshape(2 * k, 2 * k))
            out[i, 0], out[i, 1] = combine(p, n, k, live)


def section(base, bit, rank, own, other, ws):
    count, _, n, k = own.shape
    shape = jax.ShapeDtypeStruct(own.shape, BF16)
    return call(
        functools.partial(section_body, base),
        [bit, rank], [own, other, *ws], [shape] * len(ws),
        16 * count * n * k * k * len(ws), 2 << 20,
    )


def outward_body(dtype, quarter, order, *refs):
    levels, w, out, xs = refs[:-3], refs[-3], refs[-2], refs[-1]
    n = xs.shape[1] // 2
    rhs = slice(quarter * n, quarter * n + n)
    f = 0
    for level in levels:
        for i in range(level.shape[0]):
            real, imag = level[i, 0, rhs], level[i, 1, rhs]
            xs[f, :n] = jnp.concatenate([real, -imag], 1)
            xs[f, n:] = jnp.concatenate([imag, real], 1)
            f += 1
    step = 256
    piece = w.shape[4] // 4
    for p in range(2):

        def body(i, carry):
            start = pl.multiple_of(order[p] * piece + i * step, step)
            rows = pl.ds(start, step)
            acc = jnp.zeros((2 * n, step), F32)
            for f in range(xs.shape[0]):
                acc += nt(xs[f], jnp.concatenate([w[0, 0, f, 0, rows], w[0, 0, f, 1, rows]], 1))
            to = pl.ds(pl.multiple_of(i * step, step), step)
            out[p, 0, :, to] = acc[:n].astype(dtype)
            out[p, 1, :, to] = acc[n:].astype(dtype)
            return carry

        lax.fori_loop(0, piece // step, body, 0)


def outward(dtype, order, quarter, levels, w):
    _, _, n, k = levels[0].shape
    q = n // 2
    far = w.shape[2]
    piece = w.shape[4] // 4
    return call(
        functools.partial(outward_body, dtype, quarter),
        [order], [*levels, w],
        jax.ShapeDtypeStruct((2, 2, q, piece), dtype),
        8 * far * q * k * piece * 2, 4 << 20,
        [pltpu.VMEM((far, 2 * q, 2 * k), BF16)],
    )


def gather(color, block):
    one, two = ("x", "y") if color == 0 else ("y", "x")
    below = ring(block, one, 1)
    above = ring(block, one, -1)
    far_r = ring(below[:, :1], one, 1)
    far_i = ring(above[:, 1:], one, -1)
    line = jnp.concatenate([block, below, above, jnp.concatenate([far_r, far_i], 1)], 0)
    below = ring(line, two, 1)
    above = ring(line, two, -1)
    far_lo = ring(below[:2], two, 1)
    far_hi = ring(above[2:], two, -1)
    mine = [line, below, above, far_lo, far_hi]
    return mine + [swap(v, "grp", 1) for v in mine]


def on_device(
    incident,
    near_blocks,
    near_mask,
    far_source,
    far_rank,
    basis_in,
    section_one,
    section_two,
    basis_out,
):
    _, nrhs, rows = incident.shape
    leaf = near_blocks.shape[3]
    far = basis_in.shape[2]
    q = nrhs // 4
    member = lax.axis_index("mem")
    gidx = lax.axis_index("grp").reshape(1).astype(jnp.int32)

    bufs = [gather(c, incident[None, :, 2 * c * q : 2 * (c + 1) * q]) for c in range(2)]
    section_pair = swap(section_one, "mem", 1)

    axes = ("grp", "mem")
    total = lax.axis_size("grp") * lax.axis_size("mem")
    forward = [(i, i + 1) for i in range(total - 1)]
    backward = [(i + 1, i) for i in range(total - 1)]
    low = lax.ppermute(incident[:, :, rows - leaf :], axes, forward)
    high = lax.ppermute(incident[:, :, :leaf], axes, backward)
    near = near_field(near_mask, incident, low, high, near_blocks)

    bit0 = (member & 1).reshape(1).astype(jnp.int32)
    bit1 = (member >> 1).reshape(1).astype(jnp.int32)
    send_order = (member ^ jnp.array([1, 2])).astype(jnp.int32)
    keep_order = (member ^ jnp.array([0, 3])).astype(jnp.int32)
    cut = far // 2
    spans = ((0, cut), (cut, far - cut))

    pieces = []
    for h in range(2):
        two = []
        for base, count in spans:
            lev0 = level0(h, base, count, far_source, gidx, far_rank, bufs[h], basis_in)
            lev0_pair = swap(lev0, "mem", 1)
            lev1, lev1_pair = section(
                base, bit0, far_rank, lev0, lev0_pair, [section_one, section_pair]
            )
            lev1_other = swap(lev1_pair, "mem", 3)
            two += section(base, bit1, far_rank, lev1, lev1_other, [section_two])
        for quarter in range(2):
            sent = outward(BF16, send_order, quarter, two, basis_out)
            sent = swap(sent, "mem", 1)
            kept = outward(F32, keep_order, quarter, two, basis_out)
            last = (kept[1] + sent[1].astype(F32)).astype(BF16)
            last = swap(last, "mem", 3)
            at = (2 * h + quarter) * q
            pieces.append(
                (kept[0] + sent[0].astype(F32) + last.astype(F32) + near[:, at : at + q]).astype(BF16)
            )
    return jnp.concatenate(pieces, 1)


def solution(mesh):
    placed = (
        P(None, None, ("grp", "mem")),
        P(("grp", "mem"), None, None, None, None),
        P(("grp", "mem"), None),
        P(),
        P("grp", None),
        P("grp", "mem", None, None, None, None),
        P("grp", "mem", None, None, None, None),
        P("grp", "mem", None, None, None, None),
        P("grp", "mem", None, None, None, None),
    )

    return jax.shard_map(
        on_device,
        mesh=mesh,
        in_specs=placed,
        out_specs=P(None, None, ("grp", "mem")),
        check_vma=False,
    )
```

time: 274 us -> 259 us (0.945); the launches traced: 274 us -> 255 us
  waiting for transfers between devices: 180 us -> 81.1 us
  Pallas kernels: 0 us -> 68.8 us
  starting transfers between devices: 12.6 us -> 69.5 us
  matrix products: 22.1 us -> 0 us
  other arithmetic: 15.7 us -> 1.58 us
  between operations: 13.8 us -> 0.7 us
  local copies, waits for them, and re-layouts: 29.1 us -> 32.8 us
    all_gather x1 -> x0, waiting for transfers between devices: 72.8 us -> none  [on_device(): arrived = lax.all_gather(incident[None], 'grp', axis=0, tiled=True)]
    pallas_call x0 -> x21, Pallas kernels: none -> 68.8 us  [call(): pl.pallas_call(body, in_specs=[SMEM] * len(scalars) + [VMEM] * len(arrays...]
    ppermute x4 -> x45, starting transfers between devices: 12.6 us -> 69.5 us  [the longest x27 43.2 us: swap(): lax.ppermute(value, axis, [(i, i ^ mask) for i in range(lax.axis_size(axi...]
    reduce_scatter x1 -> x0, waiting for transfers between devices: 23.1 us -> none  [on_device(): far = lax.psum_scatter(terms, 'mem', scatter_dimension=2, tiled=True)]
    dot_general x28 -> x0, matrix products: 22.1 us -> none  [mult(): return jnp.einsum(form, left, right, preferred_element_type=jnp.float32)]
    unnamed x25 -> x93, local copies, waits for them, and re-layouts: 16.4 us -> 28.7 us
    gather x1 -> x0, local copies, waits for them, and re-layouts: 10.2 us -> none  [on_device(): chosen = jnp.take(arrived, sources, axis=0)]
    select_n x4 -> x0, other arithmetic: 7.95 us -> none  [the longest x2 4.01 us: on_device(): chosen = jnp.take(arrived, sources, axis=0)]
  transfers between devices with their start and end apart: 6 -> 45, of which waited for: 6 -> 16; matrix products, arithmetic and copies ran while one was open for 8% -> 1% of each run, Pallas kernels for 0% -> 27%
where the time goes in v1:
time: 259 us; the launch traced here: 255 us
  waiting for transfers between devices  81.1 us (31%)
  starting transfers between devices  69.5 us (27%)
  Pallas kernels  68.8 us (27%)
  local copies, waits for them, and re-layouts  32.8 us (13%)
    ppermute x16, waiting for transfers between devices, ring(): return lax.ppermute(value, 'grp', perm)  69.8 us
    pallas_call x21, Pallas kernels, call(): pl.pallas_call(body, in_specs=[SMEM] * len(scalars) + [VMEM] * len(arrays...  68.8 us
    ppermute x27, starting transfers between devices, swap(): lax.ppermute(value, axis, [(i, i ^ mask) for i in range(lax.axis_size(axi...  43.2 us
    unnamed x93, local copies, waits for them, and re-layouts  28.7 us
    ppermute x16, starting transfers between devices, ring(): return lax.ppermute(value, 'grp', perm)  19 us
    ppermute x27, waiting for transfers between devices, swap(): lax.ppermute(value, axis, [(i, i ^ mask) for i in range(lax.axis_size(axi...  11.3 us
    ppermute x1, starting transfers between devices, on_device(): high = lax.ppermute(incident[:, :, :leaf], axes, backward)  5.37 us
  transfers between devices with their start and end apart: 45, of which 16 were waited for; matrix products, arithmetic and copies ran while one was open for 1% of the time, Pallas kernels for 27%

profile of v1, /device:TPU:7, one launch (start us, length us, event | category | flops | bytes accessed | tf_op | source)
XLA Modules:
  0.0 254.6 jit_solution(12799158428596293857)
XLA Ops:
  3.8 5.7 %collective-permute-done.1 = bf16[1,2,128,512]{3,2,1,0:T(8,128)(2,1)S(1)} collective-permute-done((bf16[1,2,128,512]{3,2,1,0:T(8,128)(2,1)S(1)}, bf16[1,2,128,512]{3,2,1,0:T(8,128)(2,1)S(1)}, u32[]{:S(2)}, u32[]{:S(2)}) %collective-permute-start.1) | collective-permute-done | bytes 262176 | tf_op jit(solution)/shard_map/ppermute | solution.py:27
  19.0 24.0 %collective-permute-done.25 = bf16[1,2,128,512]{3,2,1,0:T(8,128)(2,1)S(1)} collective-permute-done((bf16[1,2,128,512]{3,2,1,0:T(8,128)(2,1)S(1)}, bf16[1,2,128,512]{3,2,1,0:T(8,128)(2,1)S(1)}, u32[]{:S(2)}, u32[]{:S(2)}) %collective-permute-start.25) | collective-permute-done | bytes 262176 | tf_op jit(solution)/shard_map/ppermute | solution.py:27
  43.0 3.5 %collective-permute-start.27 = (bf16[1,1,128,512]{3,2,1,0:T(8,128)(2,1)S(1)}, bf16[1,1,128,512]{3,2,1,0:T(8,128)(2,1)S(1)}, u32[]{:S(2)}, u32[]{:S(2)}) collective-permute-start(bf16[1,1,128,512]{3,2,1,0:T(8,128)(2,1)S(1)} %slice.143), channel_id=1, source_target_pairs={{0,96},{4,100},{8,104},{12,108},{16,112},{20,116},{24,120},{28,124... | collective-permute-start | bytes 393224 | tf_op jit(solution)/shard_map/ppermute | solution.py:27
  51.8 5.0 %collective-permute-start.32 = (bf16[4,2,128,512]{3,2,1,0:T(8,128)(2,1)S(1)}, bf16[4,2,128,512]{3,2,1,0:T(8,128)(2,1)S(1)}, u32[]{:S(2)}, u32[]{:S(2)}) collective-permute-start(bf16[4,2,128,512]{3,2,1,0:T(8,128)(2,1)S(1)} %maximum_maximum_fusion.1.refs_0_), channel_id=1, source_target_pairs={{0,4},{4,0},{8,12},{12,8},{16,20},{20,16},{24,28},{28,24},{32,36},... | collective-permute-start | bytes 3145736 | tf_op jit(solution)/shard_map/ppermute | solution.py:18
  60.2 12.7 %collective-permute-done.29.refs_2_ = bf16[4,2,128,512]{3,2,1,0:T(8,128)(2,1)} collective-permute-done((bf16[4,2,128,512]{3,2,1,0:T(8,128)(2,1)S(1)}, bf16[4,2,128,512]{3,2,1,0:T(8,128)(2,1)}, u32[]{:S(2)}, u32[]{:S(2)}) %collective-permute-start.29) | collective-permute-done | bytes 1048608 | tf_op jit(solution)/shard_map/ppermute | solution.py:27
  74.3 8.0 %collective-permute-done.28.refs_1_ = bf16[4,2,128,512]{3,2,1,0:T(8,128)(2,1)} collective-permute-done((bf16[4,2,128,512]{3,2,1,0:T(8,128)(2,1)S(1)}, bf16[4,2,128,512]{3,2,1,0:T(8,128)(2,1)}, u32[]{:S(2)}, u32[]{:S(2)}) %collective-permute-start.28) | collective-permute-done | bytes 1048608 | tf_op jit(solution)/shard_map/ppermute | solution.py:27
  90.5 8.3 %collective-permute-done.30.refs_3_ = bf16[2,2,128,512]{3,2,1,0:T(8,128)(2,1)} collective-permute-done((bf16[2,2,128,512]{3,2,1,0:T(8,128)(2,1)S(1)}, bf16[2,2,128,512]{3,2,1,0:T(8,128)(2,1)}, u32[]{:S(2)}, u32[]{:S(2)}) %collective-permute-start.30) | collective-permute-done | bytes 524320 | tf_op jit(solution)/shard_map/ppermute | solution.py:27
  122.3 4.0 %shard_map.112.own = bf16[7,2,128,128]{3,2,1,0:T(8,128)(2,1)} custom-call(s32[32,14]{1,0:T(8,128)S(1)} %copy.12.src, s32[1]{0:T(128)} %bitcast.2.gidx, s32[1,14]{1,0:T(1,128)S(1)} %copy-done.37, bf16[4,2,128,512]{3,2,1,0:T(8,128)(2,1)S(1)} %maximum_maximum_fusion.refs_0_, bf16[4,2,128,512]{3,2,1,0:T(8,128)(2,1)S(1)} %copy-done.13, ...), custom_call_target="tpu_custom_call" | custom-call | flops 469762048 | bytes 2097152 | tf_op jit(solution)/shard_map/pallas_call | solution.py:44
  128.0 4.0 %shard_map.109.own = bf16[7,2,128,128]{3,2,1,0:T(8,128)(2,1)} custom-call(s32[32,14]{1,0:T(8,128)S(1)} %copy.12.src, s32[1]{0:T(128)} %bitcast.2.gidx, s32[1,14]{1,0:T(1,128)S(1)} %copy-done.37, bf16[4,2,128,512]{3,2,1,0:T(8,128)(2,1)S(1)} %maximum_maximum_fusion.refs_0_, bf16[4,2,128,512]{3,2,1,0:T(8,128)(2,1)S(1)} %copy-done.13, ...), custom_call_target="tpu_custom_call" | custom-call | flops 469762048 | bytes 2097152 | tf_op jit(solution)/shard_map/pallas_call | solution.py:44
  132.1 5.9 %shard_map.120.own = bf16[7,2,128,128]{3,2,1,0:T(8,128)(2,1)} custom-call(s32[32,14]{1,0:T(8,128)S(1)} %copy.12.src, s32[1]{0:T(128)} %bitcast.2.gidx, s32[1,14]{1,0:T(1,128)S(1)} %copy-done.37, bf16[4,2,128,512]{3,2,1,0:T(8,128)(2,1)S(1)} %copy-done.7, bf16[4,2,128,512]{3,2,1,0:T(8,128)(2,1)} %collective-permute-done.28.refs_1_, ...), custom_call_target="tpu_custom_call" | custom-call | flops 469762048 | bytes 2097152 | tf_op jit(solution)/shard_map/pallas_call | solution.py:44
  142.7 5.9 %shard_map.123.own = bf16[7,2,128,128]{3,2,1,0:T(8,128)(2,1)} custom-call(s32[32,14]{1,0:T(8,128)S(1)} %copy.12.src, s32[1]{0:T(128)} %bitcast.2.gidx, s32[1,14]{1,0:T(1,128)S(1)} %copy-done.37, bf16[4,2,128,512]{3,2,1,0:T(8,128)(2,1)S(1)} %copy-done.8, bf16[4,2,128,512]{3,2,1,0:T(8,128)(2,1)} %collective-permute-done.28.refs_1_, ...), custom_call_target="tpu_custom_call" | custom-call | flops 469762048 | bytes 2097152 | tf_op jit(solution)/shard_map/pallas_call | solution.py:44
  173.2 3.4 %collective-permute-start.38 = (bf16[7,2,128,128]{3,2,1,0:T(8,128)(2,1)}, bf16[7,2,128,128]{3,2,1,0:T(8,128)(2,1)}, u32[]{:S(2)}, u32[]{:S(2)}) collective-permute-start(bf16[7,2,128,128]{3,2,1,0:T(8,128)(2,1)} %get-tuple-element.18), channel_id=1, source_target_pairs={{0,3},{1,2},{2,1},{3,0},{4,7},{5,6},{6,5},{7,4},{8,11},{9,10},{10,... | collective-permute-start | bytes 1376264 | tf_op jit(solution)/shard_map/ppermute | solution.py:18
  177.5 5.4 %collective-permute-start.21 = (bf16[2,256,256]{2,1,0:T(8,128)(2,1)}, bf16[2,256,256]{2,1,0:T(8,128)(2,1)S(1)}, u32[]{:S(2)}, u32[]{:S(2)}) collective-permute-start(bf16[2,256,256]{2,1,0:T(8,128)(2,1)} %get-tuple-element.27), channel_id=1, source_target_pairs={{1,0},{2,1},{3,2},{4,3},{5,4},{6,5},{7,6},{8,7},{9,8},{10,9},{11,1... | collective-permute-start | bytes 786440 | tf_op jit(solution)/shard_map/ppermute | solution.py:252
  192.0 5.2 %copy-done = bf16[1,1,14,2,2048,128]{5,4,3,2,1,0:T(8,128)(2,1)S(1)} copy-done((bf16[1,1,14,2,2048,128]{5,4,3,2,1,0:T(8,128)(2,1)S(1)}, bf16[1,1,14,2,2048,128]{5,4,3,2,1,0:T(8,128)(2,1)}, u32[]{:S(2)}) %copy-start) | copy-done | bytes 14680088
  197.2 3.5 %shard_map.119 = bf16[2,2,64,512]{3,2,1,0:T(8,128)(2,1)S(1)} custom-call(s32[2]{0:T(128)S(1)} %broadcast_xor_fusion.order, bf16[7,2,128,128]{3,2,1,0:T(8,128)(2,1)S(1)} %shard_map.111.refs_0_, bf16[7,2,128,128]{3,2,1,0:T(8,128)(2,1)S(1)} %shard_map.114.refs_1_, bf16[1,1,14,2,2048,128]{5,4,3,2,1,0:T(8,128)(2,1)S(1)} %copy-done), custom_call_target="tpu_custom_call" | custom-call | flops 939524096 | bytes 4194304 | tf_op jit(solution)/shard_map/pallas_call | solution.py:44
  200.8 3.5 %shard_map.116 = bf16[2,2,64,512]{3,2,1,0:T(8,128)(2,1)S(1)} custom-call(s32[2]{0:T(128)S(1)} %broadcast_xor_fusion.order, bf16[7,2,128,128]{3,2,1,0:T(8,128)(2,1)S(1)} %shard_map.111.refs_0_, bf16[7,2,128,128]{3,2,1,0:T(8,128)(2,1)S(1)} %shard_map.114.refs_1_, bf16[1,1,14,2,2048,128]{5,4,3,2,1,0:T(8,128)(2,1)S(1)} %copy-done), custom_call_target="tpu_custom_call" | custom-call | flops 939524096 | bytes 4194304 | tf_op jit(solution)/shard_map/pallas_call | solution.py:44
  205.3 3.6 %shard_map.129 = bf16[2,2,64,512]{3,2,1,0:T(8,128)(2,1)S(1)} custom-call(s32[2]{0:T(128)S(1)} %broadcast_xor_fusion.order, bf16[7,2,128,128]{3,2,1,0:T(8,128)(2,1)S(1)} %shard_map.122.refs_0_, bf16[7,2,128,128]{3,2,1,0:T(8,128)(2,1)S(1)} %shard_map.125.refs_1_, bf16[1,1,14,2,2048,128]{5,4,3,2,1,0:T(8,128)(2,1)S(1)} %bitcast.40), custom_call_target="tpu_custom_call" | custom-call | flops 939524096 | bytes 4194304 | tf_op jit(solution)/shard_map/pallas_call | solution.py:44
  208.9 3.5 %shard_map.127 = bf16[2,2,64,512]{3,2,1,0:T(8,128)(2,1)S(1)} custom-call(s32[2]{0:T(128)S(1)} %broadcast_xor_fusion.order, bf16[7,2,128,128]{3,2,1,0:T(8,128)(2,1)S(1)} %shard_map.122.refs_0_, bf16[7,2,128,128]{3,2,1,0:T(8,128)(2,1)S(1)} %shard_map.125.refs_1_, bf16[1,1,14,2,2048,128]{5,4,3,2,1,0:T(8,128)(2,1)S(1)} %bitcast.40), custom_call_target="tpu_custom_call" | custom-call | flops 939524096 | bytes 4194304 | tf_op jit(solution)/shard_map/pallas_call | solution.py:44
  214.0 3.5 %shard_map.128 = f32[2,2,64,512]{3,2,1,0:T(8,128)S(1)} custom-call(s32[2]{0:T(128)S(1)} %multiply_xor_fusion.order, bf16[7,2,128,128]{3,2,1,0:T(8,128)(2,1)S(1)} %shard_map.122.refs_0_, bf16[7,2,128,128]{3,2,1,0:T(8,128)(2,1)S(1)} %shard_map.125.refs_1_, bf16[1,1,14,2,2048,128]{5,4,3,2,1,0:T(8,128)(2,1)S(1)} %bitcast.40), custom_call_target="tpu_custom_call" | custom-call | flops 939524096 | bytes 4194304 | tf_op jit(solution)/shard_map/pallas_call | solution.py:44
  217.5 3.5 %shard_map.126 = f32[2,2,64,512]{3,2,1,0:T(8,128)S(1)} custom-call(s32[2]{0:T(128)S(1)} %multiply_xor_fusion.order, bf16[7,2,128,128]{3,2,1,0:T(8,128)(2,1)S(1)} %shard_map.122.refs_0_, bf16[7,2,128,128]{3,2,1,0:T(8,128)(2,1)S(1)} %shard_map.125.refs_1_, bf16[1,1,14,2,2048,128]{5,4,3,2,1,0:T(8,128)(2,1)S(1)} %bitcast.40), custom_call_target="tpu_custom_call" | custom-call | flops 939524096 | bytes 4194304 | tf_op jit(solution)/shard_map/pallas_call | solution.py:44
  221.0 3.5 %shard_map.118 = f32[2,2,64,512]{3,2,1,0:T(8,128)S(1)} custom-call(s32[2]{0:T(128)S(1)} %multiply_xor_fusion.order, bf16[7,2,128,128]{3,2,1,0:T(8,128)(2,1)S(1)} %shard_map.111.refs_0_, bf16[7,2,128,128]{3,2,1,0:T(8,128)(2,1)S(1)} %shard_map.114.refs_1_, bf16[1,1,14,2,2048,128]{5,4,3,2,1,0:T(8,128)(2,1)S(1)} %bitcast.40), custom_call_target="tpu_custom_call" | custom-call | flops 939524096 | bytes 4194304 | tf_op jit(solution)/shard_map/pallas_call | solution.py:44
  224.6 3.5 %shard_map.115 = f32[2,2,64,512]{3,2,1,0:T(8,128)S(1)} custom-call(s32[2]{0:T(128)S(1)} %multiply_xor_fusion.order, bf16[7,2,128,128]{3,2,1,0:T(8,128)(2,1)S(1)} %shard_map.111.refs_0_, bf16[7,2,128,128]{3,2,1,0:T(8,128)(2,1)S(1)} %shard_map.114.refs_1_, bf16[1,1,14,2,2048,128]{5,4,3,2,1,0:T(8,128)(2,1)S(1)} %bitcast.40), custom_call_target="tpu_custom_call" | custom-call | flops 939524096 | bytes 4194304 | tf_op jit(solution)/shard_map/pallas_call | solution.py:44
  229.7 5.4 %collective-permute-start.44 = (bf16[2,64,512]{2,1,0:T(8,128)(2,1)S(1)}, bf16[2,64,512]{2,1,0:T(8,128)(2,1)S(1)}, u32[]{:S(2)}, u32[]{:S(2)}) collective-permute-start(bf16[2,64,512]{2,1,0:T(8,128)(2,1)S(1)} %fusion.19), channel_id=1, source_target_pairs={{0,3},{1,2},{2,1},{3,0},{4,7},{5,6},{6,5},{7,4},{8,11},{9,10},{10,... | collective-permute-start | bytes 393224 | tf_op jit(solution)/shard_map/ppermute | solution.py:18
  237.5 7.2 %collective-permute-start.42 = (bf16[2,64,512]{2,1,0:T(8,128)(2,1)S(1)}, bf16[2,64,512]{2,1,0:T(8,128)(2,1)S(1)}, u32[]{:S(2)}, u32[]{:S(2)}) collective-permute-start(bf16[2,64,512]{2,1,0:T(8,128)(2,1)S(1)} %fusion.18), channel_id=1, source_target_pairs={{0,3},{1,2},{2,1},{3,0},{4,7},{5,6},{6,5},{7,4},{8,11},{9,10},{10,... | collective-permute-start | bytes 393224 | tf_op jit(solution)/shard_map/ppermute | solution.py:18
  (201 shorter events, 112.0 us)
Async XLA Ops:
  14.8 45.0 %collective-permute-start.5 = (bf16[4,2,128,512]{3,2,1,0:T(8,128)(2,1)S(1)}, bf16[4,2,128,512]{3,2,1,0:T(8,128)(2,1)S(1)}, u32[]{:S(2)}, u32[]{:S(2)}) collective-permute-start(bf16[4,2,128,512]{3,2,1,0:T(8,128)(2,1)S(1)} %maximum_maximum_fusion.refs_0_), channel_id=1, source_target_pairs={{0,96},{4,100},{8,104},{12,108},{16,112},{20,116},{24,120},{28,124... | collective-permute-start | bytes 3145736 | tf_op jit(solution)/shard_map/ppermute | solution.py:27
  17.6 25.5 %collective-permute-start.25 = (bf16[1,2,128,512]{3,2,1,0:T(8,128)(2,1)S(1)}, bf16[1,2,128,512]{3,2,1,0:T(8,128)(2,1)S(1)}, u32[]{:S(2)}, u32[]{:S(2)}) collective-permute-start(bf16[1,2,128,512]{3,2,1,0:T(8,128)(2,1)S(1)} %get-tuple-element.26), channel_id=1, source_target_pairs={{0,96},{4,100},{8,104},{12,108},{16,112},{20,116},{24,120},{28,124... | collective-permute-start | bytes 786440 | tf_op jit(solution)/shard_map/ppermute | solution.py:27
  18.0 28.5 %collective-permute-start.24 = (bf16[1,2,128,512]{3,2,1,0:T(8,128)(2,1)S(1)}, bf16[1,2,128,512]{3,2,1,0:T(8,128)(2,1)S(1)}, u32[]{:S(2)}, u32[]{:S(2)}) collective-permute-start(bf16[1,2,128,512]{3,2,1,0:T(8,128)(2,1)S(1)} %get-tuple-element.26), channel_id=1, source_target_pairs={{0,32},{4,36},{8,40},{12,44},{16,48},{20,52},{24,56},{28,60},{32,6... | collective-permute-start | bytes 786440 | tf_op jit(solution)/shard_map/ppermute | solution.py:27
  51.8 21.1 %collective-permute-start.29 = (bf16[4,2,128,512]{3,2,1,0:T(8,128)(2,1)S(1)}, bf16[4,2,128,512]{3,2,1,0:T(8,128)(2,1)}, u32[]{:S(2)}, u32[]{:S(2)}) collective-permute-start(bf16[4,2,128,512]{3,2,1,0:T(8,128)(2,1)S(1)} %maximum_maximum_fusion.1.refs_0_), channel_id=1, source_target_pairs={{0,24},{4,28},{8,0},{12,4},{16,8},{20,12},{24,16},{28,20},{32,56},... | collective-permute-start | bytes 3145736 | tf_op jit(solution)/shard_map/ppermute | solution.py:27
  51.8 22.3 %collective-permute-start.32 = (bf16[4,2,128,512]{3,2,1,0:T(8,128)(2,1)S(1)}, bf16[4,2,128,512]{3,2,1,0:T(8,128)(2,1)S(1)}, u32[]{:S(2)}, u32[]{:S(2)}) collective-permute-start(bf16[4,2,128,512]{3,2,1,0:T(8,128)(2,1)S(1)} %maximum_maximum_fusion.1.refs_0_), channel_id=1, source_target_pairs={{0,4},{4,0},{8,12},{12,8},{16,20},{20,16},{24,28},{28,24},{32,36},... | collective-permute-start | bytes 3145736 | tf_op jit(solution)/shard_map/ppermute | solution.py:18
  56.9 25.4 %collective-permute-start.28 = (bf16[4,2,128,512]{3,2,1,0:T(8,128)(2,1)S(1)}, bf16[4,2,128,512]{3,2,1,0:T(8,128)(2,1)}, u32[]{:S(2)}, u32[]{:S(2)}) collective-permute-start(bf16[4,2,128,512]{3,2,1,0:T(8,128)(2,1)S(1)} %maximum_maximum_fusion.1.refs_0_), channel_id=1, source_target_pairs={{0,8},{4,12},{8,16},{12,20},{16,24},{20,28},{24,0},{28,4},{32,40},... | collective-permute-start | bytes 3145736 | tf_op jit(solution)/shard_map/ppermute | solution.py:27
  59.8 25.6 %collective-permute-start.4 = (bf16[4,2,128,512]{3,2,1,0:T(8,128)(2,1)S(1)}, bf16[4,2,128,512]{3,2,1,0:T(8,128)(2,1)S(1)}, u32[]{:S(2)}, u32[]{:S(2)}) collective-permute-start(bf16[4,2,128,512]{3,2,1,0:T(8,128)(2,1)S(1)} %maximum_maximum_fusion.refs_0_), channel_id=1, source_target_pairs={{0,32},{4,36},{8,40},{12,44},{16,48},{20,52},{24,56},{28,60},{32,6... | collective-permute-start | bytes 3145736 | tf_op jit(solution)/shard_map/ppermute | solution.py:27
  59.8 28.1 %collective-permute-start.8 = (bf16[4,2,128,512]{3,2,1,0:T(8,128)(2,1)S(1)}, bf16[4,2,128,512]{3,2,1,0:T(8,128)(2,1)S(1)}, u32[]{:S(2)}, u32[]{:S(2)}) collective-permute-start(bf16[4,2,128,512]{3,2,1,0:T(8,128)(2,1)S(1)} %maximum_maximum_fusion.refs_0_), channel_id=1, source_target_pairs={{0,4},{4,0},{8,12},{12,8},{16,20},{20,16},{24,28},{28,24},{32,36},... | collective-permute-start | bytes 3145736 | tf_op jit(solution)/shard_map/ppermute | solution.py:18
  82.3 23.8 %collective-permute-start.10 = (bf16[4,2,128,512]{3,2,1,0:T(8,128)(2,1)S(1)}, bf16[4,2,128,512]{3,2,1,0:T(8,128)(2,1)S(1)}, u32[]{:S(2)}, u32[]{:S(2)}) collective-permute-start(bf16[4,2,128,512]{3,2,1,0:T(8,128)(2,1)S(1)} %collective-permute-done.5.refs_2_), channel_id=1, source_target_pairs={{0,4},{4,0},{8,12},{12,8},{16,20},{20,16},{24,28},{28,24},{32,36},... | collective-permute-start | bytes 3145736 | tf_op jit(solution)/shard_map/ppermute | solution.py:18
  90.2 18.1 %collective-permute-start.9 = (bf16[4,2,128,512]{3,2,1,0:T(8,128)(2,1)S(1)}, bf16[4,2,128,512]{3,2,1,0:T(8,128)(2,1)S(1)}, u32[]{:S(2)}, u32[]{:S(2)}) collective-permute-start(bf16[4,2,128,512]{3,2,1,0:T(8,128)(2,1)S(1)} %collective-permute-done.4.refs_1_), channel_id=1, source_target_pairs={{0,4},{4,0},{8,12},{12,8},{16,20},{20,16},{24,28},{28,24},{32,36},... | collective-permute-start | bytes 3145736 | tf_op jit(solution)/shard_map/ppermute | solution.py:18
  98.8 49.8 %collective-permute-start.14 = (bf16[1,1,14,2,128,256]{5,4,3,2,1,0:T(8,128)(2,1)S(1)}, bf16[1,1,14,2,128,256]{5,4,3,2,1,0:T(8,128)(2,1)}, u32[]{:S(2)}, u32[]{:S(2)}) collective-permute-start(bf16[1,1,14,2,128,256]{5,4,3,2,1,0:T(8,128)(2,1)S(1)} %copy-done.4), channel_id=1, source_target_pairs={{0,1},{1,0},{2,3},{3,2},{4,5},{5,4},{6,7},{7,6},{8,9},{9,8},{10,11... | collective-permute-start | bytes 5505032 | tf_op jit(solution)/shard_map/ppermute | solution.py:18
  106.0 26.0 %collective-permute-start.34 = (bf16[4,2,128,512]{3,2,1,0:T(8,128)(2,1)}, bf16[4,2,128,512]{3,2,1,0:T(8,128)(2,1)}, u32[]{:S(2)}, u32[]{:S(2)}) collective-permute-start(bf16[4,2,128,512]{3,2,1,0:T(8,128)(2,1)} %collective-permute-done.29.refs_2_), channel_id=1, source_target_pairs={{0,4},{4,0},{8,12},{12,8},{16,20},{20,16},{24,28},{28,24},{32,36},... | collective-permute-start | bytes 3145736 | tf_op jit(solution)/shard_map/ppermute | solution.py:18
  107.1 25.0 %collective-permute-start.33 = (bf16[4,2,128,512]{3,2,1,0:T(8,128)(2,1)}, bf16[4,2,128,512]{3,2,1,0:T(8,128)(2,1)}, u32[]{:S(2)}, u32[]{:S(2)}) collective-permute-start(bf16[4,2,128,512]{3,2,1,0:T(8,128)(2,1)} %collective-permute-done.28.refs_1_), channel_id=1, source_target_pairs={{0,4},{4,0},{8,12},{12,8},{16,20},{20,16},{24,28},{28,24},{32,36},... | collective-permute-start | bytes 3145736 | tf_op jit(solution)/shard_map/ppermute | solution.py:18
  109.4 22.7 %collective-permute-start.35 = (bf16[2,2,128,512]{3,2,1,0:T(8,128)(2,1)}, bf16[2,2,128,512]{3,2,1,0:T(8,128)(2,1)}, u32[]{:S(2)}, u32[]{:S(2)}) collective-permute-start(bf16[2,2,128,512]{3,2,1,0:T(8,128)(2,1)} %collective-permute-done.30.refs_3_), channel_id=1, source_target_pairs={{0,4},{4,0},{8,12},{12,8},{16,20},{20,16},{24,28},{28,24},{32,36},... | collective-permute-start | bytes 1572872 | tf_op jit(solution)/shard_map/ppermute | solution.py:18
  126.3 23.2 %collective-permute-start.16 = (bf16[7,2,128,128]{3,2,1,0:T(8,128)(2,1)}, bf16[7,2,128,128]{3,2,1,0:T(8,128)(2,1)}, u32[]{:S(2)}, u32[]{:S(2)}) collective-permute-start(bf16[7,2,128,128]{3,2,1,0:T(8,128)(2,1)} %shard_map.112.own), channel_id=1, source_target_pairs={{0,1},{1,0},{2,3},{3,2},{4,5},{5,4},{6,7},{7,6},{8,9},{9,8},{10,11... | collective-permute-start | bytes 1376264 | tf_op jit(solution)/shard_map/ppermute | solution.py:18
  132.0 27.4 %collective-permute-start.13 = (bf16[7,2,128,128]{3,2,1,0:T(8,128)(2,1)}, bf16[7,2,128,128]{3,2,1,0:T(8,128)(2,1)}, u32[]{:S(2)}, u32[]{:S(2)}) collective-permute-start(bf16[7,2,128,128]{3,2,1,0:T(8,128)(2,1)} %shard_map.109.own), channel_id=1, source_target_pairs={{0,1},{1,0},{2,3},{3,2},{4,5},{5,4},{6,7},{7,6},{8,9},{9,8},{10,11... | collective-permute-start | bytes 1376264 | tf_op jit(solution)/shard_map/ppermute | solution.py:18
  138.0 31.2 %collective-permute-start.37 = (bf16[7,2,128,128]{3,2,1,0:T(8,128)(2,1)}, bf16[7,2,128,128]{3,2,1,0:T(8,128)(2,1)}, u32[]{:S(2)}, u32[]{:S(2)}) collective-permute-start(bf16[7,2,128,128]{3,2,1,0:T(8,128)(2,1)} %shard_map.120.own), channel_id=1, source_target_pairs={{0,1},{1,0},{2,3},{3,2},{4,5},{5,4},{6,7},{7,6},{8,9},{9,8},{10,11... | collective-permute-start | bytes 1376264 | tf_op jit(solution)/shard_map/ppermute | solution.py:18
  148.6 34.3 %collective-permute-start.39 = (bf16[7,2,128,128]{3,2,1,0:T(8,128)(2,1)}, bf16[7,2,128,128]{3,2,1,0:T(8,128)(2,1)S(1)}, u32[]{:S(2)}, u32[]{:S(2)}) collective-permute-start(bf16[7,2,128,128]{3,2,1,0:T(8,128)(2,1)} %shard_map.123.own), channel_id=1, source_target_pairs={{0,1},{1,0},{2,3},{3,2},{4,5},{5,4},{6,7},{7,6},{8,9},{9,8},{10,11... | collective-permute-start | bytes 1376264 | tf_op jit(solution)/shard_map/ppermute | solution.py:18
  152.8 32.8 %collective-permute-start.17 = (bf16[7,2,128,128]{3,2,1,0:T(8,128)(2,1)}, bf16[7,2,128,128]{3,2,1,0:T(8,128)(2,1)}, u32[]{:S(2)}, u32[]{:S(2)}) collective-permute-start(bf16[7,2,128,128]{3,2,1,0:T(8,128)(2,1)} %get-tuple-element.16), channel_id=1, source_target_pairs={{0,3},{1,2},{2,1},{3,0},{4,7},{5,6},{6,5},{7,4},{8,11},{9,10},{10,... | collective-permute-start | bytes 1376264 | tf_op jit(solution)/shard_map/ppermute | solution.py:18
  163.4 25.6 %collective-permute-start.15 = (bf16[7,2,128,128]{3,2,1,0:T(8,128)(2,1)}, bf16[7,2,128,128]{3,2,1,0:T(8,128)(2,1)}, u32[]{:S(2)}, u32[]{:S(2)}) collective-permute-start(bf16[7,2,128,128]{3,2,1,0:T(8,128)(2,1)} %get-tuple-element.14), channel_id=1, source_target_pairs={{0,3},{1,2},{2,1},{3,0},{4,7},{5,6},{6,5},{7,4},{8,11},{9,10},{10,... | collective-permute-start | bytes 1376264 | tf_op jit(solution)/shard_map/ppermute | solution.py:18
  177.5 67.4 %collective-permute-start.21 = (bf16[2,256,256]{2,1,0:T(8,128)(2,1)}, bf16[2,256,256]{2,1,0:T(8,128)(2,1)S(1)}, u32[]{:S(2)}, u32[]{:S(2)}) collective-permute-start(bf16[2,256,256]{2,1,0:T(8,128)(2,1)} %get-tuple-element.27), channel_id=1, source_target_pairs={{1,0},{2,1},{3,2},{4,3},{5,4},{6,5},{7,6},{8,7},{9,8},{10,9},{11,1... | collective-permute-start | bytes 786440 | tf_op jit(solution)/shard_map/ppermute | solution.py:252
  185.4 18.9 %collective-permute-start.40 = (bf16[7,2,128,128]{3,2,1,0:T(8,128)(2,1)S(1)}, bf16[7,2,128,128]{3,2,1,0:T(8,128)(2,1)S(1)}, u32[]{:S(2)}, u32[]{:S(2)}) collective-permute-start(bf16[7,2,128,128]{3,2,1,0:T(8,128)(2,1)S(1)} %get-tuple-element.20), channel_id=1, source_target_pairs={{0,3},{1,2},{2,1},{3,0},{4,7},{5,6},{6,5},{7,4},{8,11},{9,10},{10,... | collective-permute-start | bytes 1376264 | tf_op jit(solution)/shard_map/ppermute | solution.py:18
  185.6 62.1 %collective-permute-start.20 = (bf16[2,256,256]{2,1,0:T(8,128)(2,1)S(1)}, bf16[2,256,256]{2,1,0:T(8,128)(2,1)S(1)}, u32[]{:S(2)}, u32[]{:S(2)}) collective-permute-start(bf16[2,256,256]{2,1,0:T(8,128)(2,1)S(1)} %copy-done.39), channel_id=1, source_target_pairs={{0,1},{1,2},{2,3},{3,4},{4,5},{5,6},{6,7},{7,8},{8,9},{9,10},{10,1... | collective-permute-start | bytes 786440 | tf_op jit(solution)/shard_map/ppermute | solution.py:251
  229.7 21.2 %collective-permute-start.44 = (bf16[2,64,512]{2,1,0:T(8,128)(2,1)S(1)}, bf16[2,64,512]{2,1,0:T(8,128)(2,1)S(1)}, u32[]{:S(2)}, u32[]{:S(2)}) collective-permute-start(bf16[2,64,512]{2,1,0:T(8,128)(2,1)S(1)} %fusion.19), channel_id=1, source_target_pairs={{0,3},{1,2},{2,1},{3,0},{4,7},{5,6},{6,5},{7,4},{8,11},{9,10},{10,... | collective-permute-start | bytes 393224 | tf_op jit(solution)/shard_map/ppermute | solution.py:18
  (67 other events, 647.0 us)
